TPU v7x, 256 devices: a whole 4x4x8 slice. The times are simulated.
256 devices in a mesh: req: 32 (over z, x), tp: 8 (over y, core).
Axes of the slice: x: 4, y: 4, z: 8, core: 2. Of those that a mesh axis runs over, the one named last changes fastest.
Arguments:
- hidden_in: bfloat16 [32768, 2048], P('req'), may hold values from -6 to 6
- qkv_weight: bfloat16 [2048, 3, 2048], P(None, None, 'tp'), may hold values from -0.125 to 0.125
- out_weight: bfloat16 [2048, 2048], P('tp'), may hold values from -1.5 to 1.5
- kv_pool: bfloat16 [512, 2, 128, 2048], P('req', None, None, 'tp'), may hold values from -48 to 48
- cached_len: int32 [32], replicated, may hold values from 3585 to 4096, as said below
- page_slot: int32 [32, 32], replicated, may hold values from 0 to 15
- page_holder: int32 [32, 32, 1], replicated, may hold values from 0 to 31; in each aligned block of 32 rows (0 to 31, 32 to 63, ..., all dimensions but the last counted through in order) at most 2 rows name the same one
- cont_flag: int32 [32], replicated, may hold values 0 or 1
Outputs:
- attn_out: bfloat16 [32768, 2048], P(('req', 'tp'))
Inputs may be any that keep to these rules, and one draw needn't show every extreme that they name: `page_holder`: within the table entries of the requests of one index of req (aligned blocks of 1 request), no holder is named more than 2 times. `cached_len`: A cached length of 4096 occurs in every draw. `page_slot`: page slot k of holder h is row h * 16 + k of kv_pool.
All inputs are finite; a program needn't handle non-finite values.
Results may differ from a plain program's by a relative error of at most 0.02.
Values may be sent and summed in bfloat16 or wider, within the bound.
A program may use at most 128 MiB of HBM per device.

v0:
```python
import jax
import jax.numpy as jnp
from jax import lax
from jax.sharding import PartitionSpec as P

HD = 128
NEW = 1024
PAGE = 128
MAXP = 32


def rotate(feature, position):
    half_width = feature.shape[-1] // 2
    indices = jnp.arange(half_width).astype(jnp.float32)
    inverse = jnp.exp(indices * (-2.0 / feature.shape[-1]) * jnp.log(jnp.float32(10000.0)))
    angles = position[:, None, None] * inverse[None, None, :]
    cosine = jnp.cos(angles)
    sine_part = jnp.sin(angles)
    first_half = feature[..., :half_width]
    second_half = feature[..., half_width:]
    return jnp.concatenate(
        [
            first_half * cosine - second_half * sine_part,
            second_half * cosine + first_half * sine_part,
        ],
        axis=-1,
    )


def attend_block(query_part, keys_part, values_part, allowed):
    scores = jnp.einsum(
        "qd,kd->qk", query_part, keys_part, preferred_element_type=jnp.float32
    ) * HD ** (-0.5)
    scores = jnp.where(allowed, scores, -1e30)
    row_top = jnp.max(scores, axis=-1)
    weights = jnp.where(allowed, jnp.exp(scores - row_top[:, None]), 0.0)
    row_total = jnp.sum(weights, axis=-1)
    summed = jnp.einsum(
        "qk,kd->qd", weights.astype(jnp.bfloat16), values_part, preferred_element_type=jnp.float32
    )
    return (summed, row_top, row_total)


def body(hidden_in, qkv_weight, out_weight, kv_pool, cached_len, page_slot, page_holder, cont_flag):
    req_count = lax.axis_size("req")
    tp_count = lax.axis_size("tp")
    req_index = lax.axis_index("req")
    local_reqs = hidden_in.shape[0] // NEW
    local_width = qkv_weight.shape[2]
    local_heads = local_width // HD
    table_block = local_reqs * MAXP
    capacity = max(2, 2 * table_block // req_count)
    cache_span = MAXP * PAGE
    holder_rows = page_holder[:, :, 0]
    held_here = holder_rows == req_index
    ranking = jnp.cumsum(held_here.astype(jnp.int32), axis=1) - 1
    picked = held_here[:, :, None] & (ranking[:, :, None] == jnp.arange(capacity)[None, None, :])
    send_slots = jnp.sum(jnp.where(picked, page_slot[:, :, None], 0), axis=1)
    outgoing = kv_pool[send_slots]
    lengths = lax.dynamic_slice_in_dim(cached_len, req_index * local_reqs, local_reqs)
    flags = lax.dynamic_slice_in_dim(cont_flag, req_index * local_reqs, local_reqs)
    live_len = lengths * flags
    token_rows = hidden_in.astype(jnp.float32)
    centre = jnp.mean(token_rows, axis=-1, keepdims=True)
    centred = token_rows - centre
    spread = jnp.mean(centred * centred, axis=-1, keepdims=True)
    normed = (centred * lax.rsqrt(spread + 1e-05)).astype(jnp.bfloat16)
    united_qkv = jnp.einsum("td,dcf->tcf", normed, qkv_weight, preferred_element_type=jnp.float32)
    positions = (live_len[:, None] + jnp.arange(NEW)[None, :]).astype(jnp.float32).reshape(-1)
    query_rot = rotate(united_qkv[:, 0].reshape(-1, local_heads, HD), positions).astype(
        jnp.bfloat16
    )
    new_key = rotate(united_qkv[:, 1].reshape(-1, local_heads, HD), positions).astype(jnp.bfloat16)
    new_value = united_qkv[:, 2].reshape(-1, local_heads, HD).astype(jnp.bfloat16)
    row_count = local_reqs * NEW
    block_rows = min(512, NEW)
    req_blocks = NEW // block_rows
    row_blocks = row_count // block_rows
    work_items = local_heads * row_blocks
    query_heads = query_rot.transpose(1, 0, 2)
    new_places = jnp.arange(NEW)[None, :]

    def block_place(index):
        head = index // row_blocks
        block = index % row_blocks
        owner = block // req_blocks
        query_pos = block % req_blocks * block_rows + jnp.arange(block_rows)
        query_part = lax.dynamic_slice(
            query_heads, (head, block * block_rows, 0), (1, block_rows, HD)
        )[0]
        return (head, owner, query_pos, query_part)

    incoming = lax.all_to_all(outgoing, "req", split_axis=0, concat_axis=0, tiled=True)
    own_holders = lax.dynamic_index_in_dim(holder_rows, req_index, 0, keepdims=False)
    same_holder = own_holders[:, None] == own_holders[None, :]
    earlier = jnp.arange(table_block)[None, :] < jnp.arange(table_block)[:, None]
    own_rank = jnp.sum((same_holder & earlier).astype(jnp.int32), axis=1)
    fetched = incoming.reshape(req_count * capacity, 2, PAGE, local_width)[
        own_holders * capacity + own_rank
    ]
    fetched = fetched.reshape(local_reqs, MAXP, 2, PAGE, local_width)
    cache_key = fetched[:, :, 0].reshape(local_reqs, cache_span, local_heads, HD)
    cache_value = fetched[:, :, 1].reshape(local_reqs, cache_span, local_heads, HD)
    keys_all = jnp.concatenate(
        [cache_key, new_key.reshape(local_reqs, NEW, local_heads, HD)], axis=1
    )
    values_all = jnp.concatenate(
        [cache_value, new_value.reshape(local_reqs, NEW, local_heads, HD)], axis=1
    )

    def joined_block(index):
        head, owner, query_pos, query_part = block_place(index)
        keys_part = lax.dynamic_slice(
            keys_all, (owner, 0, head, 0), (1, cache_span + NEW, 1, HD)
        ).reshape(cache_span + NEW, HD)
        values_part = lax.dynamic_slice(
            values_all, (owner, 0, head, 0), (1, cache_span + NEW, 1, HD)
        ).reshape(cache_span + NEW, HD)
        live_one = lax.dynamic_index_in_dim(live_len, owner, 0, keepdims=False)
        cache_ok = jnp.broadcast_to(
            jnp.arange(cache_span)[None, :] < live_one, (block_rows, cache_span)
        )
        allowed = jnp.concatenate([cache_ok, new_places <= query_pos[:, None]], axis=1)
        summed, row_top, row_total = attend_block(query_part, keys_part, values_part, allowed)
        return (summed / row_total[:, None]).astype(jnp.bfloat16)

    blocks_out = lax.map(joined_block, jnp.arange(work_items))
    attended = (
        blocks_out.reshape(local_heads, row_count, HD)
        .transpose(1, 0, 2)
        .reshape(row_count, local_width)
    )
    share_rows = row_count // tp_count
    head_term = jnp.dot(attended, out_weight, preferred_element_type=jnp.float32)
    summed_rows = lax.psum(head_term.astype(jnp.bfloat16), "tp")
    result = lax.dynamic_slice_in_dim(summed_rows, lax.axis_index("tp") * share_rows, share_rows, 0)
    return result


def solution(mesh):
    in_specs = (
        P("req", None),
        P(None, None, "tp"),
        P("tp", None),
        P("req", None, None, "tp"),
        P(),
        P(),
        P(),
        P(),
    )
    out_specs = P(("req", "tp"), None)
    return jax.shard_map(body, mesh=mesh, in_specs=in_specs, out_specs=out_specs, check_vma=False)
```

profile of v0, /device:TPU:2, one launch (start us, length us, event | category | flops | bytes accessed | tf_op | source)
XLA Modules:
  0.0 384.3 jit_solution(15847027432307803292)
XLA Ops:
  6.5 0.9 broadcast_compare_fusion
  7.4 0.2 reduce_window_sum.14
  7.6 0.8 select_reduce_fusion
  8.5 0.1 copy.39
  8.6 0.1 reshape.226
  8.7 7.0 %gather_fusion = bf16[64,2,128,256]{3,2,1,0:T(8,128)(2,1)} fusion(bf16[16,2,128,256]{3,2,1,0:T(8,128)(2,1)} %param.13, s32[1024]{0:T(1024)S(1)} %pad_clamp_fusion.1), kind=kCustom, calls=%fused_computation | custom fusion | bytes 16777472 | tf_op jit(solution)/shard_map/gather | solution.py:59
  15.7 11.8 %all-to-all-start = ((bf16[32,2,2,128,256]{4,3,2,1,0:T(8,128)(2,1)}), bf16[32,2,2,128,256]{4,3,2,1,0:T(8,128)(2,1)}, u32[]{:S(2)}, u32[]{:S(2)}) async-start(bf16[32,2,2,128,256]{4,3,2,1,0:T(8,128)(2,1)} %bitcast.83), calls=%async_computation | async-start | bytes 16777216 | tf_op jit(solution)/shard_map/all_to_all | solution.py:93
  27.6 0.7 dynamic_slice.43
  28.2 0.6 dynamic_slice.42
  28.9 2.8 convert_reduce_fusion
  31.7 1.2 fusion.39
  32.9 4.0 %fusion.42 = f32[1024,3,256]{0,2,1:T(8,128)S(1)} fusion(bf16[2048,3,256]{2,0,1:T(8,128)(2,1)S(1)} %copy-done, bf16[1024,2048]{1,0:T(8,128)(2,1)S(1)} %copy-done.2, f32[1024]{0:T(1024)S(1)} %add_rsqrt_fusion, f32[1024]{0:T(1024)S(1)} %broadcast_multiply_fusion), kind=kOutput, calls=%fused_computation.34 | convolution fusion | flops 3229614080 | bytes 10493952 | tf_op jit(solution)/shard_map/td,dcf->tcf/dot_general | solution.py:68
  37.0 1.6 copy-done.5
  38.7 1.0 copy.44
  39.7 1.8 fusion.55
  41.5 0.9 fusion.56
  42.4 0.3 copy.51
  42.8 0.9 fusion.57
  43.7 0.3 copy.49
  44.0 1.4 copy.50
  45.4 2.4 copy.48
  49.1 0.7 fusion.51
  49.7 0.2 convert_reduce_fusion.1
  49.9 0.7 fusion.50
  50.6 1.9 multiply_cosine_fusion
  52.5 2.8 fusion.46
  55.3 1.1 maximum_bitcast_fusion
  56.4 160.8 %all-to-all-done = bf16[32,2,2,128,256]{4,3,2,1,0:T(8,128)(2,1)} async-done(((bf16[32,2,2,128,256]{4,3,2,1,0:T(8,128)(2,1)}), bf16[32,2,2,128,256]{4,3,2,1,0:T(8,128)(2,1)}, u32[]{:S(2)}, u32[]{:S(2)}) %all-to-all-start) | async-done | bytes 8388640 | tf_op jit(solution)/shard_map/all_to_all | solution.py:93
  217.2 6.1 %gather_fusion.1 = bf16[32,2,128,256]{3,2,1,0:T(8,128)(2,1)} fusion(bf16[64,2,128,256]{3,2,1,0:T(8,128)(2,1)} %bitcast.6, s32[1024]{0:T(1024)S(1)} %pad_clamp_fusion), kind=kCustom, calls=%fused_computation.1 | custom fusion | bytes 8388736 | tf_op jit(solution)/shard_map/gather | solution.py:98
  223.4 4.7 %fusion.54 = (bf16[1,32,1,128,256]{4,3,2,1,0:T(8,128)(2,1)}, bf16[1,32,1,128,256]{4,3,2,1,0:T(8,128)(2,1)}) fusion(bf16[1,32,2,128,256]{4,3,2,1,0:T(8,128)(2,1)} %bitcast.84), kind=kLoop, calls=%fused_computation.74 | loop fusion | bytes 8388608 | tf_op jit(solution)/shard_map/slice | solution.py:103
  228.0 2.5 reshape_squeeze.16
  230.6 1.6 copy.43
  232.2 2.5 reshape_squeeze.14
  234.8 0.3 copy.42
  235.1 1.3 copy-done.3
  236.3 0.1 copy-done.6
  236.4 0.2 copy-done.7
  236.6 0.2 copy-done.8
  236.7 2.3 maximum_maximum_fusion
  239.0 46.8 %while.13 = (s32[]{:T(128)}, bf16[4,512,128]{2,1,0:T(8,128)(2,1)}, s32[1]{0:T(128)}, s32[4]{0:T(128)S(1)}, bf16[2,1024,128]{2,1,0:T(8,128)(2,1)}, /*index=5*/bf1...) while((s32[]{:T(128)}, bf16[4,512,128]{2,1,0:T(8,128)(2,1)}, ...), condition=%wide.region_8.9_spmd.clone, body=%wide.region_5.8_spmd.clone.sunk | while | flops 1374293504 | bytes 46968904 | solution.py:127
  239.0 0.7 dynamic_slice.87
  242.5 0.4 iota_compare_fusion.6
  242.9 2.9 fusion.68
  245.8 2.5 fusion.69
  248.3 2.4 fusion.70
  250.7 0.7 dynamic_slice.87
  254.2 0.4 iota_compare_fusion.6
  254.6 2.9 fusion.68
  257.5 2.5 fusion.69
  260.0 2.4 fusion.70
  262.4 0.7 dynamic_slice.87
  265.9 0.4 iota_compare_fusion.6
  266.3 2.9 fusion.68
  269.2 2.5 fusion.69
  271.7 2.4 fusion.70
  274.1 0.7 dynamic_slice.87
  277.6 0.4 iota_compare_fusion.6
  278.0 2.9 fusion.68
  280.9 2.5 fusion.69
  283.4 2.4 fusion.70
  285.8 2.0 copy.45
  287.8 4.8 %convolution_convert_fusion = bf16[1024,2048]{1,0:T(8,128)(2,1)} fusion(bf16[1024,256]{0,1:T(8,128)(2,1)} %bitcast.87, bf16[256,2048]{1,0:T(8,128)(2,1)} %param.12), kind=kOutput, calls=%fused_computation.37 | convolution fusion | flops 1075838976 | bytes 5767168 | tf_op jit(solution)/shard_map/dot_general | solution.py:134
  292.6 83.0 %all-reduce.2.cloned.1.call-done = bf16[1024,2048]{1,0:T(8,128)(2,1)} async-done(((bf16[1024,2048]{1,0:T(8,128)(2,1)}), bf16[1024,2048]{1,0:T(8,128)(2,1)}) %all-reduce.2.cloned.1.call-update) | async-done | bytes 4194320 | tf_op jit(solution)/shard_map/psum | solution.py:135
  375.6 1.9 constant_dynamic-slice_fusion.1
  (49 shorter events, 0.3 us)
Async XLA Ops:
  6.5 26.4 %copy-start = (bf16[2048,3,256]{2,0,1:T(8,128)(2,1)S(1)}, bf16[2048,3,256]{2,0,1:T(8,128)(2,1)}, u32[]{:S(2)}) copy-start(bf16[2048,3,256]{2,0,1:T(8,128)(2,1)} %param.11) | copy-start | bytes 9437188
  15.7 11.9 %copy-start.9 = (s32[32]{0:T(128)S(1)}, s32[32]{0:T(128)}, u32[]{:S(2)}) copy-start(s32[32]{0:T(128)} %param.17) | copy-start | bytes 388
  15.7 12.6 %copy-start.10 = (s32[32]{0:T(128)S(1)}, s32[32]{0:T(128)}, u32[]{:S(2)}) copy-start(s32[32]{0:T(128)} %param.14) | copy-start | bytes 388
  15.7 201.5 %all-to-all-start = ((bf16[32,2,2,128,256]{4,3,2,1,0:T(8,128)(2,1)}), bf16[32,2,2,128,256]{4,3,2,1,0:T(8,128)(2,1)}, u32[]{:S(2)}, u32[]{:S(2)}) async-start(bf16[32,2,2,128,256]{4,3,2,1,0:T(8,128)(2,1)} %bitcast.83), calls=%async_computation | async-start | bytes 16777216 | tf_op jit(solution)/shard_map/all_to_all | solution.py:93
  27.5 348.1 %all-reduce.2.cloned.1.call-start = ((), (), s32[]{:S(2)}) async-start(), calls=%async_computation.1 | async-start | bytes 8388608 | tf_op jit(solution)/shard_map/psum | solution.py:135
  27.5 4.1 %copy-start.2 = (bf16[1024,2048]{1,0:T(8,128)(2,1)S(1)}, bf16[1024,2048]{1,0:T(8,128)(2,1)}, u32[]{:S(2)}) copy-start(bf16[1024,2048]{1,0:T(8,128)(2,1)} %param.10) | copy-start | bytes 12582916
  37.0 1.7 copy-start.5
  234.7 1.6 copy-start.3
  234.7 1.7 copy-start.6
  234.8 1.8 copy-start.7
  234.8 2.0 copy-start.8
  245.8 2.5 copy-start.4
  257.5 2.5 copy-start.4
  269.2 2.5 copy-start.4
  280.9 2.5 copy-start.4
  287.8 89.6 %copy-start.1 = (bf16[2048,3,256]{2,0,1:T(8,128)(2,1)S(1)}, bf16[2048,3,256]{2,0,1:T(8,128)(2,1)}, u32[]{:S(2)}) copy-start(bf16[2048,3,256]{2,0,1:T(8,128)(2,1)} %param.11) | copy-start | bytes 9437188
Sparse Core Ops, SparseCore 0:
  292.7 82.8 all-reduce.1
where the time goes:
time: 385 us; the launch traced here: 384 us
  waiting for transfers between devices  244 us (63%)
  local copies, waits for them, and re-layouts  46 us (12%)
  matrix products  30 us (8%)
  other arithmetic  26.4 us (7%)
  between operations  14.9 us (4%)
  starting transfers between devices  11.8 us (3%)
  loops' own time  11.4 us (3%)
    all_to_all x1, waiting for transfers between devices, body(): lax.all_to_all(outgoing, 'req', split_axis=0, concat_axis=0, tiled=True)  161 us
    psum x1, waiting for transfers between devices, body(): summed_rows = lax.psum(head_term.astype(jnp.bfloat16), 'tp')  83 us
    all_to_all x1, starting transfers between devices, body(): lax.all_to_all(outgoing, 'req', split_axis=0, concat_axis=0, tiled=True)  11.8 us
    dot_general x4, matrix products, attend_block(): jnp.einsum('qd,kd->qk', query_part, keys_part, preferred_element_type=jnp...  11.5 us
    another operation x1, loops' own time, body(): blocks_out = lax.map(joined_block, jnp.arange(work_items))  11.4 us
    reduce_sum x4, other arithmetic, attend_block(): row_total = jnp.sum(weights, axis=-1)  9.99 us
    dot_general x4, matrix products, attend_block(): jnp.einsum('qk,kd->qd', weights.astype(jnp.bfloat16), values_part, prefer...  9.69 us
    unnamed x24, local copies, waits for them, and re-layouts  7.73 us
  transfers between devices with their start and end apart: 2, of which 2 were waited for; matrix products, arithmetic and copies ran while one was open for 7% of the time, Pallas kernels for 0%

commit v1 on v0

--- a/solution.py
+++ b/solution.py
@@ -132,7 +132,7 @@
     )
     share_rows = row_count // tp_count
     head_term = jnp.dot(attended, out_weight, preferred_element_type=jnp.float32)
-    summed_rows = lax.psum(head_term.astype(jnp.bfloat16), "tp")
+    summed_rows = jnp.sum(lax.all_gather(head_term.astype(jnp.bfloat16), "tp"), axis=0)
     result = lax.dynamic_slice_in_dim(summed_rows, lax.axis_index("tp") * share_rows, share_rows, 0)
     return result
 

time: 385 us -> 481 us (1.25)
  waiting for transfers between devices: 244 us -> 325 us
  other arithmetic: 26.4 us -> 40.9 us
    all_gather x0 -> x1, waiting for transfers between devices: none -> 164 us  [body(): lax.all_gather(head_term.astype(jnp.bfloat16), 'tp')]
    psum x1 -> x0, waiting for transfers between devices: 83 us -> none  [body(): summed_rows = lax.psum(head_term.astype(jnp.bfloat16), 'tp')]
    reduce_sum x0 -> x1, other arithmetic: none -> 14.5 us  [body(): jnp.sum(lax.all_gather(head_term.astype(jnp.bfloat16), 'tp'), axis=0)]
  transfers between devices with their start and end apart: 2 -> 2, of which waited for: 2 -> 2; matrix products, arithmetic and copies ran while one was open for 7% -> 5% of each run, Pallas kernels for 0% -> 0%
where the time goes in v1:
time: 481 us; the launch traced here: 479 us
  waiting for transfers between devices  325 us (68%)
  local copies, waits for them, and re-layouts  45.2 us (9%)
  other arithmetic  40.9 us (9%)
  matrix products  29.8 us (6%)
  between operations  14.9 us (3%)
  starting transfers between devices  11.8 us (2%)
  loops' own time  11.4 us (2%)
    all_gather x1, waiting for transfers between devices, body(): lax.all_gather(head_term.astype(jnp.bfloat16), 'tp')  164 us
    all_to_all x1, waiting for transfers between devices, body(): lax.all_to_all(outgoing, 'req', split_axis=0, concat_axis=0, tiled=True)  161 us
    reduce_sum x1, other arithmetic, body(): jnp.sum(lax.all_gather(head_term.astype(jnp.bfloat16), 'tp'), axis=0)  14.5 us
    all_to_all x1, starting transfers between devices, body(): lax.all_to_all(outgoing, 'req', split_axis=0, concat_axis=0, tiled=True)  11.8 us
    dot_general x4, matrix products, attend_block(): jnp.einsum('qd,kd->qk', query_part, keys_part, preferred_element_type=jnp...  11.5 us
    another operation x1, loops' own time, body(): blocks_out = lax.map(joined_block, jnp.arange(work_items))  11.4 us
    reduce_sum x4, other arithmetic, attend_block(): row_total = jnp.sum(weights, axis=-1)  9.99 us
    dot_general x4, matrix products, attend_block(): jnp.einsum('qk,kd->qd', weights.astype(jnp.bfloat16), values_part, prefer...  9.69 us
  transfers between devices with their start and end apart: 2, of which 2 were waited for; matrix products, arithmetic and copies ran while one was open for 5% of the time, Pallas kernels for 0%

profile of v1, /device:TPU:2, one launch (start us, length us, event | category | flops | bytes accessed | tf_op | source)
XLA Modules:
  0.0 478.7 jit_solution(9160877212912081910)
XLA Ops:
  6.5 0.9 broadcast_compare_fusion
  7.4 0.2 reduce_window_sum.14
  7.6 0.8 select_reduce_fusion
  8.5 0.1 copy.39
  8.6 0.1 reshape.226
  8.7 7.0 %gather_fusion = bf16[64,2,128,256]{3,2,1,0:T(8,128)(2,1)} fusion(bf16[16,2,128,256]{3,2,1,0:T(8,128)(2,1)} %param.13, s32[1024]{0:T(1024)S(1)} %pad_clamp_fusion.1), kind=kCustom, calls=%fused_computation | custom fusion | bytes 16777472 | tf_op jit(solution)/shard_map/gather | solution.py:59
  15.7 11.8 %all-to-all-start = ((bf16[32,2,2,128,256]{4,3,2,1,0:T(8,128)(2,1)}), bf16[32,2,2,128,256]{4,3,2,1,0:T(8,128)(2,1)}, u32[]{:S(2)}, u32[]{:S(2)}) async-start(bf16[32,2,2,128,256]{4,3,2,1,0:T(8,128)(2,1)} %bitcast.85), calls=%async_computation | async-start | bytes 16777216 | tf_op jit(solution)/shard_map/all_to_all | solution.py:93
  27.6 0.7 dynamic_slice.43
  28.2 0.6 dynamic_slice.42
  28.9 2.8 convert_reduce_fusion
  31.7 1.2 fusion.39
  32.9 4.0 fusion.42
  37.0 1.6 copy-done.5
  38.7 1.0 copy.44
  39.7 1.8 fusion.55
  41.5 0.9 fusion.56
  42.4 0.3 copy.51
  42.8 0.9 fusion.57
  43.7 0.3 copy.49
  44.0 1.4 copy.50
  45.4 2.4 copy.48
  49.1 0.7 fusion.51
  49.7 0.2 convert_reduce_fusion.1
  49.9 0.7 fusion.50
  50.6 1.9 multiply_cosine_fusion
  52.5 2.8 fusion.46
  55.3 1.1 maximum_bitcast_fusion
  56.4 160.8 %all-to-all-done = bf16[32,2,2,128,256]{4,3,2,1,0:T(8,128)(2,1)} async-done(((bf16[32,2,2,128,256]{4,3,2,1,0:T(8,128)(2,1)}), bf16[32,2,2,128,256]{4,3,2,1,0:T(8,128)(2,1)}, u32[]{:S(2)}, u32[]{:S(2)}) %all-to-all-start) | async-done | bytes 8388640 | tf_op jit(solution)/shard_map/all_to_all | solution.py:93
  217.2 6.1 %gather_fusion.1 = bf16[32,2,128,256]{3,2,1,0:T(8,128)(2,1)} fusion(bf16[64,2,128,256]{3,2,1,0:T(8,128)(2,1)} %bitcast.6, s32[1024]{0:T(1024)S(1)} %pad_clamp_fusion), kind=kCustom, calls=%fused_computation.1 | custom fusion | bytes 8388736 | tf_op jit(solution)/shard_map/gather | solution.py:98
  223.4 4.7 fusion.54
  228.0 2.5 reshape_squeeze.16
  230.6 1.6 copy.43
  232.2 2.5 reshape_squeeze.14
  234.8 0.3 copy.42
  235.1 1.3 copy-done.3
  236.4 0.2 copy-done.7
  236.6 0.2 copy-done.8
  236.7 2.3 maximum_maximum_fusion
  239.0 46.8 %while.13 = (s32[]{:T(128)}, bf16[4,512,128]{2,1,0:T(8,128)(2,1)}, s32[1]{0:T(128)}, s32[4]{0:T(128)S(1)}, bf16[2,1024,128]{2,1,0:T(8,128)(2,1)}, /*index=5*/bf1...) while((s32[]{:T(128)}, bf16[4,512,128]{2,1,0:T(8,128)(2,1)}, ...), condition=%wide.region_8.9_spmd.clone, body=%wide.region_5.8_spmd.clone.sunk | while | flops 1374293504 | bytes 46968904 | solution.py:127
  239.0 0.7 dynamic_slice.87
  242.5 0.4 iota_compare_fusion.6
  242.9 2.9 fusion.68
  245.8 2.5 fusion.69
  248.3 2.4 fusion.70
  250.7 0.7 dynamic_slice.87
  254.2 0.4 iota_compare_fusion.6
  254.6 2.9 fusion.68
  257.5 2.5 fusion.69
  260.0 2.4 fusion.70
  262.4 0.7 dynamic_slice.87
  265.9 0.4 iota_compare_fusion.6
  266.3 2.9 fusion.68
  269.2 2.5 fusion.69
  271.7 2.4 fusion.70
  274.1 0.7 dynamic_slice.87
  277.6 0.4 iota_compare_fusion.6
  278.0 2.9 fusion.68
  280.9 2.5 fusion.69
  283.4 2.4 fusion.70
  285.8 1.2 copy.45
  287.1 4.6 convolution_convert_fusion
  291.7 163.8 %all-gather.3.cloned.1.call-done = bf16[8192,2048]{1,0:T(8,128)(2,1)} async-done(((bf16[1024,2048]{1,0:T(8,128)(2,1)}), bf16[8192,2048]{1,0:T(8,128)(2,1)}) %all-gather.3.cloned.1.call-update) | async-done | bytes 33554448 | tf_op jit(solution)/shard_map/all_gather | solution.py:135
  455.5 14.5 %reduce_sum.70 = bf16[1024,2048]{1,0:T(8,128)(2,1)} reduce(bf16[8,1024,2048]{2,1,0:T(8,128)(2,1)} %bitcast.84, bf16[]{:T(256)} %constant.133.clone.1), dimensions={0}, to_apply=%region_9.10 | reduce | flops 14680064 | bytes 37748736 | tf_op jit(solution)/shard_map/reduce_sum | solution.py:135
  470.0 1.9 constant_dynamic-slice_fusion.1
  (50 shorter events, 0.4 us)
Async XLA Ops:
  6.5 26.4 %copy-start = (bf16[2048,3,256]{2,0,1:T(8,128)(2,1)S(1)}, bf16[2048,3,256]{2,0,1:T(8,128)(2,1)}, u32[]{:S(2)}) copy-start(bf16[2048,3,256]{2,0,1:T(8,128)(2,1)} %param.11) | copy-start | bytes 9437188
  15.7 11.9 %copy-start.9 = (s32[32]{0:T(128)S(1)}, s32[32]{0:T(128)}, u32[]{:S(2)}) copy-start(s32[32]{0:T(128)} %param.17) | copy-start | bytes 388
  15.7 12.6 %copy-start.10 = (s32[32]{0:T(128)S(1)}, s32[32]{0:T(128)}, u32[]{:S(2)}) copy-start(s32[32]{0:T(128)} %param.14) | copy-start | bytes 388
  15.7 201.5 %all-to-all-start = ((bf16[32,2,2,128,256]{4,3,2,1,0:T(8,128)(2,1)}), bf16[32,2,2,128,256]{4,3,2,1,0:T(8,128)(2,1)}, u32[]{:S(2)}, u32[]{:S(2)}) async-start(bf16[32,2,2,128,256]{4,3,2,1,0:T(8,128)(2,1)} %bitcast.85), calls=%async_computation | async-start | bytes 16777216 | tf_op jit(solution)/shard_map/all_to_all | solution.py:93
  27.5 428.0 %all-gather.3.cloned.1.call-start = ((), (), s32[]{:S(2)}) async-start(), calls=%async_computation.1 | async-start | bytes 37748736 | tf_op jit(solution)/shard_map/all_gather | solution.py:135
  27.5 4.1 copy-start.2
  37.0 1.7 copy-start.5
  234.7 1.6 copy-start.3
  234.7 1.7 copy-start.6
  234.8 1.8 copy-start.7
  234.8 2.0 copy-start.8
  245.8 2.5 copy-start.4
  257.5 2.5 copy-start.4
  269.2 2.5 copy-start.4
  280.9 2.5 copy-start.4
  455.5 16.4 %copy-start.1 = (bf16[2048,3,256]{2,0,1:T(8,128)(2,1)S(1)}, bf16[2048,3,256]{2,0,1:T(8,128)(2,1)}, u32[]{:S(2)}) copy-start(bf16[2048,3,256]{2,0,1:T(8,128)(2,1)} %param.11) | copy-start | bytes 9437188
Sparse Core Ops, SparseCore 0:
  291.8 163.6 all-gather.2
